TPU v7x, 32 devices: a whole 2x2x4 slice. The times are simulated.
32 devices in a mesh: prop: 8 (over y, x, core), width: 4 (over z).
Axes of the slice: x: 2, y: 2, z: 4, core: 2. Of those that a mesh axis runs over, the one named last changes fastest.
Arguments:
- e_forward: float32 [3, 128, 128, 512], P(None, 'prop', 'width'), may hold values from -6 to 6
- h_forward: float32 [3, 128, 128, 512], P(None, 'prop', 'width'), may hold values from -6 to 6
- e_adjoint: float32 [3, 128, 128, 512], P(None, 'prop', 'width'), may hold values from -6 to 6
- h_adjoint: float32 [3, 128, 128, 512], P(None, 'prop', 'width'), may hold values from -6 to 6
- material: int32 [128, 128, 512], P('prop', 'width'), may hold values from 0 to 3
- eps_table: float32 [4], replicated, may hold values from 1.5 to 12
- omega: float32 [12], replicated, may hold values from 0.2 to 3
- mode_profile: float32 [64, 128, 512], P(None, 'width'), may hold values from -0.0234375 to 0.0234375
- port_order: int32 [64], replicated, may hold values from 0 to 63, each once
- owner: int32 [65536, 1], P(('prop', 'width')), may hold values from 0 to 31; in each aligned block of 2048 rows (0 to 2047, 2048 to 4095, ...) at most 128 rows name the same one
- segment: int32 [65536], P(('prop', 'width')), may hold values from 0 to 7
Outputs:
- e_forward_end: float32 [3, 128, 128, 512], P(None, 'prop', 'width')
- e_adjoint_end: float32 [3, 128, 128, 512], P(None, 'prop', 'width')
- port_amp: float32 [8, 64, 24], P('prop', 'width')
- seg_grad: float32 [256, 128], P(('prop', 'width'))
Inputs may be any that keep to these rules, and one draw needn't show every extreme that they name: Among the 2048 blocks of one device, no owner is named more than 128 times, a bound that some block reaches. `port_order`: each port appears once.
All inputs are finite; a program needn't handle non-finite values.
Results may differ from a plain program's by a relative error of at most 0.0001.
Values sent between devices are 32-bit elements; how exact they have to be, the bound alone decides.
A program may use at most 128 MiB of HBM per device.

v0:
```python
import functools

import jax
import jax.numpy as jnp
from jax import lax
from jax.experimental import pallas as pl
from jax.experimental.pallas import tpu as pltpu
from jax.sharding import PartitionSpec as P

NMAT = 4
ZBLK = 128
SEG_DEV = 8
COURANT = 0.5
GRAD_SCALE = -0.05
MESH = pl.DeviceIdType.MESH
T = 8


def kernel(
    n_prop, n_width,
    ef_in, hf_in, ea_in, ha_in, mat_in, mode_in, eps_ref, omega_ref, order_ref, idx_ref,
    ef_out, ea_out, port_out, seg_out,
    E, H, E2, mat, coef, mode, hx_halo, hy_halo, ysend, G, OH, pacc,
    seg_part, recv1, part2, recv2, ordered, recvp,
    load_sem, out_sem, send_sem, recv_sem, red_send, red_recv,
):
    CX, CY, NZ = mat.shape
    TILES = CY // T
    ZB = NZ // ZBLK
    p = lax.axis_index("prop")
    w = lax.axis_index("width")
    e_in, h_in = (ef_in, ea_in), (hf_in, ha_in)

    loads_e = [pltpu.make_async_copy(e_in[r], E.at[r], load_sem.at[r]) for r in range(2)]
    loads_h = [pltpu.make_async_copy(h_in[r], H.at[r], load_sem.at[2 + r]) for r in range(2)]
    load_mat = pltpu.make_async_copy(mat_in, mat, load_sem.at[4])
    load_mode = pltpu.make_async_copy(mode_in, mode, load_sem.at[5])
    for c in loads_e + loads_h + [load_mat, load_mode]:
        c.start()

    barrier = pltpu.get_barrier_semaphore()
    for d in range(1, n_prop):
        pl.semaphore_signal(barrier, inc=1, device_id=(lax.rem(p + d, n_prop), w), device_id_type=MESH)
    for d in range(1, n_width):
        pl.semaphore_signal(barrier, inc=1, device_id=(p, lax.rem(w + d, n_width)), device_id_type=MESH)

    def sem_of(r, phase, direction):
        return (r * 4 + phase) * 2 + direction

    def face_copy(r, phase, direction):
        ahead = phase % 2 == 0
        step = -1 if ahead else 1
        if direction == 0:
            if phase == 0:
                src = e_in[r].at[pl.ds(1, 2), 0]
            elif ahead:
                src = E.at[r, pl.ds(1, 2), 0]
            else:
                src = H.at[r, pl.ds(1, 2), CX - 1]
            dst = hx_halo.at[r, phase]
            dev = (jnp.clip(p + step, 0, n_prop - 1), w)
            may_send = p > 0 if ahead else p < n_prop - 1
            may_recv = p < n_prop - 1 if ahead else p > 0
        else:
            src = ysend.at[r, phase]
            dst = hy_halo.at[r, phase]
            dev = (p, jnp.clip(w + step, 0, n_width - 1))
            may_send = w > 0 if ahead else w < n_width - 1
            may_recv = w < n_width - 1 if ahead else w > 0
        k = sem_of(r, phase, direction)
        copy = pltpu.make_async_remote_copy(
            src_ref=src, dst_ref=dst, send_sem=send_sem.at[k], recv_sem=recv_sem.at[k],
            device_id=dev, device_id_type=MESH,
        )
        return copy, may_send, may_recv

    def send(r, phase, direction):
        copy, may_send, _ = face_copy(r, phase, direction)

        @pl.when(may_send)
        def _():
            copy.start()

    def wait_send(r, phase, direction):
        copy, may_send, _ = face_copy(r, phase, direction)

        @pl.when(may_send)
        def _():
            copy.wait_send()

    def wait_recv(r, phase, direction):
        copy, _, may_recv = face_copy(r, phase, direction)

        @pl.when(may_recv)
        def _():
            copy.wait_recv()

        @pl.when(jnp.logical_not(may_recv))
        def _():
            if direction == 0:
                hx_halo[r, phase] = jnp.zeros(hx_halo.shape[2:], jnp.float32)
            else:
                hy_halo[r, phase] = jnp.zeros(hy_halo.shape[2:], jnp.float32)

    row = lax.broadcasted_iota(jnp.int32, (T, NZ), 0)
    lane = lax.broadcasted_iota(jnp.int32, (T, NZ), 1)
    row_last, row_first = row == T - 1, row == 0
    lane_last, lane_first = lane == NZ - 1, lane == 0
    zero = jnp.float32(0.0)

    def z_next(v):
        return jnp.where(lane_last, zero, pltpu.roll(v, NZ - 1, 1))

    def z_prev(v):
        return jnp.where(lane_first, zero, pltpu.roll(v, 1, 1))

    def y_next(v, nxt):
        return jnp.where(row_last, jnp.broadcast_to(nxt, v.shape), pltpu.roll(v, T - 1, 0))

    def y_prev(v, prv):
        return jnp.where(row_first, jnp.broadcast_to(prv, v.shape), pltpu.roll(v, 1, 0))

    def h_tile(r, phase, i, j, x_edge):
        rows = pl.ds(j * T, T)
        ex, ey, ez = E[r, 0, i, rows, :], E[r, 1, i, rows, :], E[r, 2, i, rows, :]
        if x_edge:
            ey_x, ez_x = hx_halo[r, phase, 0, rows, :], hx_halo[r, phase, 1, rows, :]
        else:
            ey_x, ez_x = E[r, 1, i + 1, rows, :], E[r, 2, i + 1, rows, :]
        if j == TILES - 1:
            nx, nz = hy_halo[r, phase, 0, i], hy_halo[r, phase, 1, i]
        else:
            nx, nz = E[r, 0, i, pl.ds(j * T + T, 1), :], E[r, 2, i, pl.ds(j * T + T, 1), :]
        cx = (y_next(ez, nz) - ez) - (z_next(ey) - ey)
        cy = (z_next(ex) - ex) - (ez_x - ez)
        cz = (ey_x - ey) - (y_next(ex, nx) - ex)
        H[r, 0, i, rows, :] = H[r, 0, i, rows, :] - COURANT * cx
        H[r, 1, i, rows, :] = H[r, 1, i, rows, :] - COURANT * cy
        H[r, 2, i, rows, :] = H[r, 2, i, rows, :] - COURANT * cz

    def e_tile(r, phase, i, j, x_edge):
        rows = pl.ds(j * T, T)
        hx, hy, hz = H[r, 0, i, rows, :], H[r, 1, i, rows, :], H[r, 2, i, rows, :]
        if x_edge:
            hy_x, hz_x = hx_halo[r, phase, 0, rows, :], hx_halo[r, phase, 1, rows, :]
        else:
            hy_x, hz_x = H[r, 1, i - 1, rows, :], H[r, 2, i - 1, rows, :]
        if j == 0:
            px, pz = hy_halo[r, phase, 0, i], hy_halo[r, phase, 1, i]
        else:
            px, pz = H[r, 0, i, pl.ds(j * T - 1, 1), :], H[r, 2, i, pl.ds(j * T - 1, 1), :]
        k = coef[i, rows, :]
        old = [E[r, c, i, rows, :] for c in range(3)]
        new = [
            old[0] + k * ((hz - y_prev(hz, pz)) - (hy - z_prev(hy))),
            old[1] + k * ((hx - z_prev(hx)) - (hz - hz_x)),
            old[2] + k * ((hy - hy_x) - (hx - y_prev(hx, px))),
        ]
        out = E if phase == 1 else E2
        for c in range(3):
            out[r, c, i, rows, :] = new[c]
        if phase == 3 and r == 1:
            total = None
            for c in range(3):
                term = E[0, c, i, rows, :] * new[c] + E2[0, c, i, rows, :] * old[c]
                total = term if total is None else total + term
            g = GRAD_SCALE * total
            for z in range(ZB):
                G[pl.ds((i * CY + j * T) * ZB + z, T, stride=ZB), :] = g[:, z * ZBLK:(z + 1) * ZBLK]

    def h_inner(r, phase):
        def body(i, carry):
            for j in range(TILES - 1):
                h_tile(r, phase, i, j, False)
            return carry

        lax.fori_loop(0, CX - 1, body, 0)

    def h_edge(r, phase, save):
        def body(i, carry):
            h_tile(r, phase, i, TILES - 1, False)
            for n, c in enumerate((0, 2)):
                ysend[r, phase + 1, n, i] = H[r, c, i, pl.ds(CY - 1, 1), :]
            return carry

        for j in range(TILES):
            h_tile(r, phase, CX - 1, j, True)
        for n, c in enumerate((0, 2)):
            ysend[r, phase + 1, n, CX - 1] = H[r, c, CX - 1, pl.ds(CY - 1, 1), :]
        send(r, phase + 1, 0)
        lax.fori_loop(0, CX - 1, body, 0)
        send(r, phase + 1, 1)

    def e_inner(r, phase):
        def body(i, carry):
            for j in range(1, TILES):
                e_tile(r, phase, i, j, False)
            return carry

        lax.fori_loop(1, CX, body, 0)

    def e_edge(r, phase):
        more = phase == 1

        def body(i, carry):
            e_tile(r, phase, i, 0, False)
            if more:
                for n, c in enumerate((0, 2)):
                    ysend[r, phase + 1, n, i] = E[r, c, i, pl.ds(0, 1), :]
            return carry

        for j in range(TILES):
            e_tile(r, phase, 0, j, True)
        if more:
            for n, c in enumerate((0, 2)):
                ysend[r, phase + 1, n, 0] = E[r, c, 0, pl.ds(0, 1), :]
            send(r, phase + 1, 0)
        lax.fori_loop(1, CX, body, 0)
        if more:
            send(r, phase + 1, 1)

    def ports(fields, t):
        plane = [fields[0, 2, 0, pl.ds(j * T, T), :] for j in range(TILES)]

        def body(q, carry):
            acc = None
            for j in range(TILES):
                m = mode[q, pl.ds(j * T, T), :] * plane[j]
                acc = m if acc is None else acc + m
            total = acc[:, :ZBLK]
            for z in range(1, ZB):
                total = total + acc[:, z * ZBLK:(z + 1) * ZBLK]
            pacc[pl.ds(pl.multiple_of(q * T, T), T), pl.ds(t * ZBLK, ZBLK)] = total
            return carry

        lax.fori_loop(0, mode.shape[0], body, 0)

    pl.semaphore_wait(barrier, n_prop + n_width - 2)
    for r in range(2):
        send(r, 0, 0)
    for r in range(2):
        loads_e[r].wait()

        def rows_out(i, carry, r=r):
            for n, c in enumerate((0, 2)):
                ysend[r, 0, n, i] = E[r, c, i, pl.ds(0, 1), :]
            return carry

        lax.fori_loop(0, CX, rows_out, 0)
        send(r, 0, 1)

    load_mat.wait()

    def coef_body(i, carry):
        inv = [COURANT / jnp.full((T, NZ), eps_ref[m], jnp.float32) for m in range(NMAT)]
        for j in range(TILES):
            v = mat[i, pl.ds(j * T, T), :]
            out = jnp.zeros((T, NZ), jnp.float32)
            for m in range(NMAT):
                out = jnp.where(v == m, inv[m], out)
            coef[i, pl.ds(j * T, T), :] = out
        return carry

    lax.fori_loop(0, CX, coef_body, 0)

    loads_h[0].wait()
    h_inner(0, 0)
    loads_h[1].wait()
    h_inner(1, 0)

    for step in range(2):
        a, b = 2 * step, 2 * step + 1
        if step == 1:
            for r in range(2):
                h_inner(r, a)
        for r in range(2):
            wait_recv(r, a, 0)
            wait_recv(r, a, 1)
            if step == 1:
                wait_send(r, 1, 0)
            h_edge(r, a, True)
        for r in range(2):
            e_inner(r, b)
        if step == 0:
            def hot(s, carry):
                base = pl.multiple_of(s * 32, 32)
                mine = lax.broadcasted_iota(jnp.int32, (32, idx_ref.shape[1]), 0) + base
                OH[pl.ds(base, 32), :] = jnp.where(mine == idx_ref[...], 1.0, 0.0).astype(jnp.bfloat16)
                return carry

            lax.fori_loop(0, OH.shape[0] // 32, hot, 0)
        for r in range(2):
            wait_recv(r, b, 0)
            wait_recv(r, b, 1)
            if step == 0:
                pass
            e_edge(r, b)
            if step == 1:
                pltpu.make_async_copy(E2.at[r], (ef_out, ea_out)[r], out_sem.at[r]).start()
        if step == 0:
            load_mode.wait()
            ports(E, 0)
    seg = None
    K = 512
    for k in range(G.shape[0] // K):
        g = G[pl.ds(k * K, K), :]
        hi = g.astype(jnp.bfloat16)
        lo = (g - hi.astype(jnp.float32)).astype(jnp.bfloat16)
        part = OH[:, pl.ds(k * K, K)]
        term = jnp.dot(part, hi, preferred_element_type=jnp.float32) + jnp.dot(part, lo, preferred_element_type=jnp.float32)
        seg = term if seg is None else seg + term
    seg_part[...] = seg.reshape(seg_part.shape)

    def width_copies(d):
        to = lax.rem(w + d, n_width)
        seg_c = pltpu.make_async_remote_copy(
            src_ref=seg_part.at[:, to], dst_ref=recv1.at[d - 1],
            send_sem=red_send.at[d - 1], recv_sem=red_recv.at[d - 1],
            device_id=(p, to), device_id_type=MESH)
        port_c = pltpu.make_async_remote_copy(
            src_ref=ordered.at[to], dst_ref=recvp.at[d - 1],
            send_sem=red_send.at[n_width - 1 + d - 1], recv_sem=red_recv.at[n_width - 1 + d - 1],
            device_id=(p, to), device_id_type=MESH)
        return seg_c, port_c

    for d in range(1, n_width):
        width_copies(d)[0].start()

    ports(E2, 1)
    n_ports = mode.shape[0]
    port_of = lax.broadcasted_iota(jnp.int32, (n_ports, n_ports * T), 1) // T
    pick = jnp.where(port_of == order_ref[...], 1.0, 0.0).astype(jnp.bfloat16)
    v = pacc[...]
    hi = v.astype(jnp.bfloat16)
    lo = (v - hi.astype(jnp.float32)).astype(jnp.bfloat16)
    o = jnp.dot(pick, hi, preferred_element_type=jnp.float32) + jnp.dot(pick, lo, preferred_element_type=jnp.float32)
    ordered[...] = o.reshape(ordered.shape)
    for d in range(1, n_width):
        width_copies(d)[1].start()

    for d in range(1, n_width):
        width_copies(d)[0].wait_recv()
    total = seg_part[:, w]
    for d in range(1, n_width):
        total = total + recv1[d - 1]
    part2[...] = total

    base = 2 * (n_width - 1)

    def prop_copy(d):
        to = lax.rem(p + d, n_prop)
        return pltpu.make_async_remote_copy(
            src_ref=part2.at[to], dst_ref=recv2.at[d - 1],
            send_sem=red_send.at[base + d - 1], recv_sem=red_recv.at[base + d - 1],
            device_id=(to, w), device_id_type=MESH)

    for d in range(1, n_prop):
        prop_copy(d).start()

    for d in range(1, n_width):
        width_copies(d)[1].wait_recv()
    mine = ordered[w]
    for d in range(1, n_width):
        mine = mine + recvp[d - 1]
    s1 = jnp.sum(mine[:, :ZBLK], axis=1, keepdims=True)
    s2 = jnp.sum(mine[:, ZBLK:], axis=1, keepdims=True)
    nf = omega_ref.shape[1]
    om = jnp.broadcast_to(omega_ref[...], (mine.shape[0], nf))
    port_out[0, :, 0:nf] = jnp.cos(om) * s1 + jnp.cos(om * 2.0) * s2
    port_out[0, :, nf:2 * nf] = -(jnp.sin(om) * s1 + jnp.sin(om * 2.0) * s2)

    for d in range(1, n_prop):
        prop_copy(d).wait_recv()
    got = part2[p]
    for d in range(1, n_prop):
        got = got + recv2[d - 1]
    seg_out[...] = got

    for r in range(2):
        for phase in range(4):
            for direction in range(2):
                if (phase, direction) != (1, 0):
                    wait_send(r, phase, direction)
    for d in range(1, n_width):
        width_copies(d)[0].wait_send()
        width_copies(d)[1].wait_send()
    for d in range(1, n_prop):
        prop_copy(d).wait_send()
    for r in range(2):
        pltpu.make_async_copy(E2.at[r], (ef_out, ea_out)[r], out_sem.at[r]).wait()


def on_device(
    n_prop, n_width,
    e_forward, h_forward, e_adjoint, h_adjoint, material, eps_table, omega,
    mode_profile, port_order, owner, segment,
):
    _, CX, CY, NZ = e_forward.shape
    blocks = owner.shape[0]
    ports = mode_profile.shape[0]
    nf = omega.shape[0]
    segs = n_prop * n_width * SEG_DEV
    idx = owner.reshape(1, blocks) * SEG_DEV + segment.reshape(1, blocks)
    anyspec = pl.BlockSpec(memory_space=pl.ANY)
    vm = pl.BlockSpec(memory_space=pltpu.VMEM)
    sm = pl.BlockSpec(memory_space=pltpu.SMEM)
    f32 = jnp.float32
    n_red = 2 * (n_width - 1) + n_prop - 1
    field = (2, 3, CX, CY, NZ)
    return pl.pallas_call(
        functools.partial(kernel, n_prop, n_width),
        out_shape=(
            jax.ShapeDtypeStruct(e_forward.shape, f32),
            jax.ShapeDtypeStruct(e_adjoint.shape, f32),
            jax.ShapeDtypeStruct((1, ports // n_width, 2 * nf), f32),
            jax.ShapeDtypeStruct((SEG_DEV, ZBLK), f32),
        ),
        in_specs=[anyspec] * 6 + [sm, vm, vm, vm],
        out_specs=(anyspec, anyspec, vm, vm),
        scratch_shapes=[
            pltpu.VMEM(field, f32),
            pltpu.VMEM(field, f32),
            pltpu.VMEM(field, f32),
            pltpu.VMEM((CX, CY, NZ), jnp.int32),
            pltpu.VMEM((CX, CY, NZ), f32),
            pltpu.VMEM((ports, CY, NZ), f32),
            pltpu.VMEM((2, 4, 2, CY, NZ), f32),
            pltpu.VMEM((2, 4, 2, CX, 1, NZ), f32),
            pltpu.VMEM((2, 4, 2, CX, 1, NZ), f32),
            pltpu.VMEM((blocks, ZBLK), f32),
            pltpu.VMEM((segs, blocks), jnp.bfloat16),
            pltpu.VMEM((ports * T, 2 * ZBLK), f32),
            pltpu.VMEM((n_prop, n_width, SEG_DEV, ZBLK), f32),
            pltpu.VMEM((n_width - 1, n_prop, SEG_DEV, ZBLK), f32),
            pltpu.VMEM((n_prop, SEG_DEV, ZBLK), f32),
            pltpu.VMEM((n_prop - 1, SEG_DEV, ZBLK), f32),
            pltpu.VMEM((n_width, ports // n_width, 2 * ZBLK), f32),
            pltpu.VMEM((n_width - 1, ports // n_width, 2 * ZBLK), f32),
            pltpu.SemaphoreType.DMA((6,)),
            pltpu.SemaphoreType.DMA((2,)),
            pltpu.SemaphoreType.DMA((16,)),
            pltpu.SemaphoreType.DMA((16,)),
            pltpu.SemaphoreType.DMA((n_red,)),
            pltpu.SemaphoreType.DMA((n_red,)),
        ],
        compiler_params=pltpu.CompilerParams(
            collective_id=0, has_side_effects=True, vmem_limit_bytes=60 * 1024 * 1024
        ),
    )(
        e_forward, h_forward, e_adjoint, h_adjoint, material, mode_profile,
        eps_table, omega.reshape(1, nf), port_order.reshape(ports, 1), idx,
    )


def solution(mesh):
    n_prop, n_width = mesh.shape["prop"], mesh.shape["width"]
    placed = (
        P(None, "prop", "width", None),
        P(None, "prop", "width", None),
        P(None, "prop", "width", None),
        P(None, "prop", "width", None),
        P("prop", "width", None),
        P(),
        P(),
        P(None, "width", None),
        P(),
        P(("prop", "width"), None),
        P(("prop", "width")),
    )
    return jax.shard_map(
        functools.partial(on_device, n_prop, n_width),
        mesh=mesh,
        in_specs=placed,
        out_specs=(
            P(None, "prop", "width", None),
            P(None, "prop", "width", None),
            P("prop", "width", None),
            P(("prop", "width"), None),
        ),
        check_vma=False,
    )
```

profile of v0, /device:TPU:0, one launch (start us, length us, event | category | flops | bytes accessed | tf_op | source)
XLA Modules:
  0.0 54.6 jit_solution(10991156234386276831)
XLA Ops:
  0.6 0.7 %broadcast_multiply_fusion = s32[2048,1]{0,1:T(1,128)S(1)} fusion(s32[2048,1]{0,1:T(1,128)} %param.20), kind=kLoop, calls=%fused_computation | loop fusion | flops 2048 | bytes 16384 | tf_op jit(solution)/shard_map/mul | solution.py:403
  1.3 1.3 %add.5 = s32[2048]{0:T(1024)} add(s32[2048]{0:T(1024)S(1)} %bitcast.5, s32[2048]{0:T(1024)} %param.21) | non-fusion elementwise | flops 2048 | bytes 24576 | tf_op jit(solution)/shard_map/add | solution.py:403
  2.6 1.4 %copy.15.order_ref = s32[64,1]{1,0:T(8,128)} copy(s32[64,1]{0,1:T(1,128)} %bitcast.6) | data formatting | bytes 512 | tf_op jit(solution)/shard_map/reshape | solution.py:451
  4.0 43.5 %shard_map.138 = (f32[3,16,32,512]{3,2,1,0:T(8,128)}, f32[3,16,32,512]{3,2,1,0:T(8,128)}, f32[1,16,24]{2,1,0:T(8,128)}, f32[8,128]{1,0:T(8,128)}) custom-call(f32[3,16,32,512]{3,2,1,0:T(8,128)} %ef_in.1, f32[3,16,32,512]{3,2,1,0:T(8,128)} %hf_in.1, f32[3,16,32,512]{3,2,1,0:T(8,128)} %ea_in.1, f32[3,16,32,512]{3,2,1,0:T(8,128)} %ha_in.1, ...), custom_call_target="tpu_custom_call" | custom-call | tf_op jit(solution)/shard_map/pallas_call | solution.py:410
  47.5 0.0 copy-start
  47.5 4.2 %copy.20 = f32[3,16,32,512]{3,2,1,0:T(8,128)} copy(f32[3,16,32,512]{3,2,1,0:T(8,128)} %get-tuple-element.8) | data formatting | bytes 6291456
  51.8 0.0 copy-done
  51.8 0.0 copy-start.1
  51.8 0.0 copy-start.2
  51.8 1.7 %copy.21 = f32[3,16,32,512]{3,2,1,0:T(8,128)} copy(f32[3,16,32,512]{3,2,1,0:T(8,128)S(1)} %copy-done) | data formatting | bytes 6291456
  53.4 0.0 copy-done.1
  53.4 0.6 %copy.22 = f32[1,16,24]{2,1,0:T(8,128)} copy(f32[1,16,24]{2,1,0:T(8,128)S(1)} %copy-done.1) | data formatting | bytes 3072
  54.0 0.0 copy-done.2
  54.0 0.6 %copy.23 = f32[8,128]{1,0:T(8,128)} copy(f32[8,128]{1,0:T(8,128)S(1)} %copy-done.2) | data formatting | bytes 8192
Async XLA Ops:
  47.5 4.3 %copy-start = (f32[3,16,32,512]{3,2,1,0:T(8,128)S(1)}, f32[3,16,32,512]{3,2,1,0:T(8,128)}, u32[]{:S(2)}) copy-start(f32[3,16,32,512]{3,2,1,0:T(8,128)} %get-tuple-element.9) | copy-start | bytes 9437188
  51.8 1.7 %copy-start.1 = (f32[1,16,24]{2,1,0:T(8,128)S(1)}, f32[1,16,24]{2,1,0:T(8,128)}, u32[]{:S(2)}) copy-start(f32[1,16,24]{2,1,0:T(8,128)} %get-tuple-element.10) | copy-start | bytes 4612
  51.8 2.3 %copy-start.2 = (f32[8,128]{1,0:T(8,128)S(1)}, f32[8,128]{1,0:T(8,128)}, u32[]{:S(2)}) copy-start(f32[8,128]{1,0:T(8,128)} %get-tuple-element.11) | copy-start | bytes 12292
where the time goes:
time: 54.9 us; the launch traced here: 54.6 us
  Pallas kernels  43.5 us (79%)
  local copies, waits for them, and re-layouts  8.47 us (15%)
  other arithmetic  2 us (4%)
  between operations  0.65 us (1%)
    pallas_call x1, Pallas kernels, on_device(): pl.pallas_call(functools.partial(kernel, n_prop, n_width), out_shape=(jax...  43.5 us
    unnamed x10, local copies, waits for them, and re-layouts  7.12 us
    reshape x1, local copies, waits for them, and re-layouts, on_device(): port_order.reshape(ports, 1)  1.36 us
    add x1, other arithmetic, on_device(): idx = owner.reshape(1, blocks) * SEG_DEV + segment.reshape(1, blocks)  1.3 us

commit v1 on v0

--- a/solution.py
+++ b/solution.py
@@ -18,11 +18,11 @@
 
 def kernel(
     n_prop, n_width,
-    ef_in, hf_in, ea_in, ha_in, mat_in, mode_in, eps_ref, omega_ref, order_ref, idx_ref,
-    ef_out, ea_out, port_out, seg_out,
-    E, H, E2, mat, coef, mode, hx_halo, hy_halo, ysend, G, OH, pacc,
+    ef_in, hf_in, ea_in, ha_in, mat_in, mode_in, eps_ref, omega_ref, order_ref, owner_ref, segment_ref,
+    E2, port_out, seg_out,
+    E, H, mat, coef, mode, hx_halo, hy_halo, ysend, G, OH, pacc, trig,
     seg_part, recv1, part2, recv2, ordered, recvp,
-    load_sem, out_sem, send_sem, recv_sem, red_send, red_recv,
+    load_sem, send_sem, recv_sem, red_send, red_recv,
 ):
     CX, CY, NZ = mat.shape
     TILES = CY // T
@@ -31,11 +31,17 @@
     w = lax.axis_index("width")
     e_in, h_in = (ef_in, ea_in), (hf_in, ha_in)
 
-    loads_e = [pltpu.make_async_copy(e_in[r], E.at[r], load_sem.at[r]) for r in range(2)]
-    loads_h = [pltpu.make_async_copy(h_in[r], H.at[r], load_sem.at[2 + r]) for r in range(2)]
-    load_mat = pltpu.make_async_copy(mat_in, mat, load_sem.at[4])
-    load_mode = pltpu.make_async_copy(mode_in, mode, load_sem.at[5])
-    for c in loads_e + loads_h + [load_mat, load_mode]:
+    def load(src, dst, k):
+        return pltpu.make_async_copy(src, dst, load_sem.at[k])
+
+    first = [[load(e_in[r].at[c, :, pl.ds(0, T), :], E.at[r, c, :, pl.ds(0, T), :], r * 6 + n)
+              for n, c in enumerate((0, 2))] for r in range(2)]
+    rest = [[load(e_in[r].at[c, :, pl.ds(T, CY - T), :], E.at[r, c, :, pl.ds(T, CY - T), :], r * 6 + 2 + n)
+             for n, c in enumerate((0, 2))] + [load(e_in[r].at[1], E.at[r, 1], r * 6 + 4)] for r in range(2)]
+    loads_h = [load(h_in[r], H.at[r], r * 6 + 5) for r in range(2)]
+    load_mat = load(mat_in, mat, 12)
+    load_mode = load(mode_in, mode, 13)
+    for c in first[0] + first[1] + rest[0] + [loads_h[0]]:
         c.start()
 
     barrier = pltpu.get_barrier_semaphore()
@@ -176,7 +182,7 @@
 
         lax.fori_loop(0, CX - 1, body, 0)
 
-    def h_edge(r, phase, save):
+    def h_edge(r, phase):
         def body(i, carry):
             h_tile(r, phase, i, TILES - 1, False)
             for n, c in enumerate((0, 2)):
@@ -222,7 +228,8 @@
     def ports(fields, t):
         plane = [fields[0, 2, 0, pl.ds(j * T, T), :] for j in range(TILES)]
 
-        def body(q, carry):
+        def body(n, carry):
+            q = order_ref[n]
             acc = None
             for j in range(TILES):
                 m = mode[q, pl.ds(j * T, T), :] * plane[j]
@@ -230,16 +237,29 @@
             total = acc[:, :ZBLK]
             for z in range(1, ZB):
                 total = total + acc[:, z * ZBLK:(z + 1) * ZBLK]
-            pacc[pl.ds(pl.multiple_of(q * T, T), T), pl.ds(t * ZBLK, ZBLK)] = total
+            pacc[n, :, pl.ds(t * ZBLK, ZBLK)] = total
             return carry
 
         lax.fori_loop(0, mode.shape[0], body, 0)
+
+    def width_copies(d):
+        to = lax.rem(w + d, n_width)
+        seg_c = pltpu.make_async_remote_copy(
+            src_ref=seg_part.at[:, to], dst_ref=recv1.at[d - 1],
+            send_sem=red_send.at[d - 1], recv_sem=red_recv.at[d - 1],
+            device_id=(p, to), device_id_type=MESH)
+        port_c = pltpu.make_async_remote_copy(
+            src_ref=ordered.at[to], dst_ref=recvp.at[d - 1],
+            send_sem=red_send.at[n_width - 1 + d - 1], recv_sem=red_recv.at[n_width - 1 + d - 1],
+            device_id=(p, to), device_id_type=MESH)
+        return seg_c, port_c
 
     pl.semaphore_wait(barrier, n_prop + n_width - 2)
     for r in range(2):
         send(r, 0, 0)
     for r in range(2):
-        loads_e[r].wait()
+        for c in first[r]:
+            c.wait()
 
         def rows_out(i, carry, r=r):
             for n, c in enumerate((0, 2)):
@@ -248,7 +268,21 @@
 
         lax.fori_loop(0, CX, rows_out, 0)
         send(r, 0, 1)
-
+    for c in rest[1] + [loads_h[1], load_mat]:
+        c.start()
+    for c in rest[0] + [loads_h[0]]:
+        c.wait()
+    h_inner(0, 0)
+    load_mode.start()
+    for c in rest[1] + [loads_h[1]]:
+        c.wait()
+    h_inner(1, 0)
+
+    om = omega_ref[...]
+    trig[0] = jnp.cos(om)
+    trig[1] = jnp.cos(om * 2.0)
+    trig[2] = jnp.sin(om)
+    trig[3] = jnp.sin(om * 2.0)
     load_mat.wait()
 
     def coef_body(i, carry):
@@ -263,41 +297,34 @@
 
     lax.fori_loop(0, CX, coef_body, 0)
 
-    loads_h[0].wait()
-    h_inner(0, 0)
-    loads_h[1].wait()
-    h_inner(1, 0)
-
-    for step in range(2):
-        a, b = 2 * step, 2 * step + 1
-        if step == 1:
-            for r in range(2):
-                h_inner(r, a)
+    for phase in range(4):
         for r in range(2):
-            wait_recv(r, a, 0)
-            wait_recv(r, a, 1)
-            if step == 1:
-                wait_send(r, 1, 0)
-            h_edge(r, a, True)
-        for r in range(2):
-            e_inner(r, b)
-        if step == 0:
+            wait_recv(r, phase, 0)
+            wait_recv(r, phase, 1)
+            if phase % 2 == 0:
+                if phase == 2:
+                    wait_send(r, 1, 0)
+                h_edge(r, phase)
+                e_inner(r, phase + 1)
+            else:
+                e_edge(r, phase)
+                if phase == 1:
+                    h_inner(r, phase + 1)
+                elif r == 0:
+                    ports(E2, 1)
+                    ordered[...] = jnp.sum(pacc[...], axis=1).reshape(ordered.shape)
+                    for d in range(1, n_width):
+                        width_copies(d)[1].start()
+        if phase == 0:
             def hot(s, carry):
                 base = pl.multiple_of(s * 32, 32)
-                mine = lax.broadcasted_iota(jnp.int32, (32, idx_ref.shape[1]), 0) + base
-                OH[pl.ds(base, 32), :] = jnp.where(mine == idx_ref[...], 1.0, 0.0).astype(jnp.bfloat16)
+                mine = lax.broadcasted_iota(jnp.int32, (32, owner_ref.shape[1]), 0) + base
+                named = owner_ref[...] * SEG_DEV + segment_ref[...]
+                OH[pl.ds(base, 32), :] = jnp.where(mine == named, 1.0, 0.0).astype(jnp.bfloat16)
                 return carry
 
             lax.fori_loop(0, OH.shape[0] // 32, hot, 0)
-        for r in range(2):
-            wait_recv(r, b, 0)
-            wait_recv(r, b, 1)
-            if step == 0:
-                pass
-            e_edge(r, b)
-            if step == 1:
-                pltpu.make_async_copy(E2.at[r], (ef_out, ea_out)[r], out_sem.at[r]).start()
-        if step == 0:
+        if phase == 1:
             load_mode.wait()
             ports(E, 0)
     seg = None
@@ -311,32 +338,8 @@
         seg = term if seg is None else seg + term
     seg_part[...] = seg.reshape(seg_part.shape)
 
-    def width_copies(d):
-        to = lax.rem(w + d, n_width)
-        seg_c = pltpu.make_async_remote_copy(
-            src_ref=seg_part.at[:, to], dst_ref=recv1.at[d - 1],
-            send_sem=red_send.at[d - 1], recv_sem=red_recv.at[d - 1],
-            device_id=(p, to), device_id_type=MESH)
-        port_c = pltpu.make_async_remote_copy(
-            src_ref=ordered.at[to], dst_ref=recvp.at[d - 1],
-            send_sem=red_send.at[n_width - 1 + d - 1], recv_sem=red_recv.at[n_width - 1 + d - 1],
-            device_id=(p, to), device_id_type=MESH)
-        return seg_c, port_c
-
     for d in range(1, n_width):
         width_copies(d)[0].start()
-
-    ports(E2, 1)
-    n_ports = mode.shape[0]
-    port_of = lax.broadcasted_iota(jnp.int32, (n_ports, n_ports * T), 1) // T
-    pick = jnp.where(port_of == order_ref[...], 1.0, 0.0).astype(jnp.bfloat16)
-    v = pacc[...]
-    hi = v.astype(jnp.bfloat16)
-    lo = (v - hi.astype(jnp.float32)).astype(jnp.bfloat16)
-    o = jnp.dot(pick, hi, preferred_element_type=jnp.float32) + jnp.dot(pick, lo, preferred_element_type=jnp.float32)
-    ordered[...] = o.reshape(ordered.shape)
-    for d in range(1, n_width):
-        width_copies(d)[1].start()
 
     for d in range(1, n_width):
         width_copies(d)[0].wait_recv()
@@ -365,9 +368,8 @@
     s1 = jnp.sum(mine[:, :ZBLK], axis=1, keepdims=True)
     s2 = jnp.sum(mine[:, ZBLK:], axis=1, keepdims=True)
     nf = omega_ref.shape[1]
-    om = jnp.broadcast_to(omega_ref[...], (mine.shape[0], nf))
-    port_out[0, :, 0:nf] = jnp.cos(om) * s1 + jnp.cos(om * 2.0) * s2
-    port_out[0, :, nf:2 * nf] = -(jnp.sin(om) * s1 + jnp.sin(om * 2.0) * s2)
+    port_out[0, :, 0:nf] = trig[0] * s1 + trig[1] * s2
+    port_out[0, :, nf:2 * nf] = -(trig[2] * s1 + trig[3] * s2)
 
     for d in range(1, n_prop):
         prop_copy(d).wait_recv()
@@ -386,8 +388,15 @@
         width_copies(d)[1].wait_send()
     for d in range(1, n_prop):
         prop_copy(d).wait_send()
-    for r in range(2):
-        pltpu.make_async_copy(E2.at[r], (ef_out, ea_out)[r], out_sem.at[r]).wait()
+
+
+def write_out(E2, port, seg, ef_out, ea_out, port_out, seg_out, sem):
+    pairs = ((E2.at[0], ef_out), (E2.at[1], ea_out), (port, port_out), (seg, seg_out))
+    copies = [pltpu.make_async_copy(src, dst, sem.at[n]) for n, (src, dst) in enumerate(pairs)]
+    for c in copies:
+        c.start()
+    for c in copies:
+        c.wait()
 
 
 def on_device(
@@ -400,25 +409,23 @@
     ports = mode_profile.shape[0]
     nf = omega.shape[0]
     segs = n_prop * n_width * SEG_DEV
-    idx = owner.reshape(1, blocks) * SEG_DEV + segment.reshape(1, blocks)
-    anyspec = pl.BlockSpec(memory_space=pl.ANY)
+    hbm = pl.BlockSpec(memory_space=pltpu.HBM)
     vm = pl.BlockSpec(memory_space=pltpu.VMEM)
     sm = pl.BlockSpec(memory_space=pltpu.SMEM)
     f32 = jnp.float32
     n_red = 2 * (n_width - 1) + n_prop - 1
     field = (2, 3, CX, CY, NZ)
-    return pl.pallas_call(
+    port_shape = (1, ports // n_width, 2 * nf)
+    E2, port, seg = pl.pallas_call(
         functools.partial(kernel, n_prop, n_width),
         out_shape=(
-            jax.ShapeDtypeStruct(e_forward.shape, f32),
-            jax.ShapeDtypeStruct(e_adjoint.shape, f32),
-            jax.ShapeDtypeStruct((1, ports // n_width, 2 * nf), f32),
-            jax.ShapeDtypeStruct((SEG_DEV, ZBLK), f32),
+            pltpu.VMEM(field, f32),
+            pltpu.VMEM(port_shape, f32),
+            pltpu.VMEM((SEG_DEV, ZBLK), f32),
         ),
-        in_specs=[anyspec] * 6 + [sm, vm, vm, vm],
-        out_specs=(anyspec, anyspec, vm, vm),
+        in_specs=[hbm] * 6 + [sm, vm, sm, vm, vm],
+        out_specs=(vm, vm, vm),
         scratch_shapes=[
-            pltpu.VMEM(field, f32),
             pltpu.VMEM(field, f32),
             pltpu.VMEM(field, f32),
             pltpu.VMEM((CX, CY, NZ), jnp.int32),
@@ -429,27 +436,41 @@
             pltpu.VMEM((2, 4, 2, CX, 1, NZ), f32),
             pltpu.VMEM((blocks, ZBLK), f32),
             pltpu.VMEM((segs, blocks), jnp.bfloat16),
-            pltpu.VMEM((ports * T, 2 * ZBLK), f32),
+            pltpu.VMEM((ports, T, 2 * ZBLK), f32),
+            pltpu.VMEM((4, 1, nf), f32),
             pltpu.VMEM((n_prop, n_width, SEG_DEV, ZBLK), f32),
             pltpu.VMEM((n_width - 1, n_prop, SEG_DEV, ZBLK), f32),
             pltpu.VMEM((n_prop, SEG_DEV, ZBLK), f32),
             pltpu.VMEM((n_prop - 1, SEG_DEV, ZBLK), f32),
             pltpu.VMEM((n_width, ports // n_width, 2 * ZBLK), f32),
             pltpu.VMEM((n_width - 1, ports // n_width, 2 * ZBLK), f32),
-            pltpu.SemaphoreType.DMA((6,)),
-            pltpu.SemaphoreType.DMA((2,)),
+            pltpu.SemaphoreType.DMA((14,)),
             pltpu.SemaphoreType.DMA((16,)),
             pltpu.SemaphoreType.DMA((16,)),
             pltpu.SemaphoreType.DMA((n_red,)),
             pltpu.SemaphoreType.DMA((n_red,)),
         ],
         compiler_params=pltpu.CompilerParams(
-            collective_id=0, has_side_effects=True, vmem_limit_bytes=60 * 1024 * 1024
+            collective_id=0, has_side_effects=True, vmem_limit_bytes=52 * 1024 * 1024
         ),
     )(
-        e_forward, h_forward, e_adjoint, h_adjoint, material, mode_profile,
-        eps_table, omega.reshape(1, nf), port_order.reshape(ports, 1), idx,
+        *(pltpu.with_memory_space_constraint(x, pltpu.HBM) for x in
+          (e_forward, h_forward, e_adjoint, h_adjoint, material, mode_profile)),
+        eps_table, omega.reshape(1, nf), port_order, owner.reshape(1, blocks), segment.reshape(1, blocks),
     )
+    return pl.pallas_call(
+        write_out,
+        out_shape=(
+            jax.ShapeDtypeStruct(e_forward.shape, f32),
+            jax.ShapeDtypeStruct(e_adjoint.shape, f32),
+            jax.ShapeDtypeStruct(port_shape, f32),
+            jax.ShapeDtypeStruct((SEG_DEV, ZBLK), f32),
+        ),
+        in_specs=[vm] * 3,
+        out_specs=(hbm, hbm, hbm, hbm),
+        scratch_shapes=[pltpu.SemaphoreType.DMA((4,))],
+        compiler_params=pltpu.CompilerParams(vmem_limit_bytes=2 * 1024 * 1024),
+    )(*(pltpu.with_memory_space_constraint(x, pltpu.VMEM) for x in (E2, port, seg)))
 
 
 def solution(mesh):

time: 54.9 us -> 46.1 us (0.84)
  local copies, waits for them, and re-layouts: 8.47 us -> 0 us
  other arithmetic: 2 us -> 0 us
  Pallas kernels: 43.5 us -> 45.2 us
    unnamed x10 -> x0, local copies, waits for them, and re-layouts: 7.12 us -> none
    pallas_call x1 -> x2, Pallas kernels: 43.5 us -> 45.2 us  [the longest x1 42.5 us: on_device(): pl.pallas_call(functools.partial(kernel, n_prop, n_width), out_shape=(plt...]
    reshape x1 -> x0, local copies, waits for them, and re-layouts: 1.36 us -> none  [on_device(): port_order.reshape(ports, 1)]
    add x1 -> x0, other arithmetic: 1.3 us -> none  [on_device(): idx = owner.reshape(1, blocks) * SEG_DEV + segment.reshape(1, blocks)]
    mul x1 -> x0, other arithmetic: 0.71 us -> none  [on_device(): idx = owner.reshape(1, blocks) * SEG_DEV + segment.reshape(1, blocks)]
where the time goes in v1:
time: 46.1 us; the launch traced here: 45.9 us
  Pallas kernels  45.2 us (98%)
  between operations  0.64 us (1%)
    pallas_call x1, Pallas kernels, on_device(): pl.pallas_call(functools.partial(kernel, n_prop, n_width), out_shape=(plt...  42.5 us
    pallas_call x1, Pallas kernels, on_device(): pl.pallas_call(write_out, out_shape=(jax.ShapeDtypeStruct(e_forward.shape...  2.74 us

profile of v1, /device:TPU:0, one launch (start us, length us, event | category | flops | bytes accessed | tf_op | source)
XLA Modules:
  0.0 45.9 jit_solution(16767824658884663054)
XLA Ops:
  0.6 42.5 %shard_map.138 = (f32[2,3,16,32,512]{4,3,2,1,0:T(8,128)S(1)}, f32[1,16,24]{2,1,0:T(8,128)S(1)}, f32[8,128]{1,0:T(8,128)S(1)}) custom-call(f32[3,16,32,512]{3,2,1,0:T(8,128)} %ef_in.1, f32[3,16,32,512]{3,2,1,0:T(8,128)} %hf_in.1, f32[3,16,32,512]{3,2,1,0:T(8,128)} %ea_in.1, f32[3,16,32,512]{3,2,1,0:T(8,128)} %ha_in.1, s32[16,32,512]{2,1,0:T(8,128)} %mat_in.1, ...), custom_call_target="tpu_custom_call" | custom-call | tf_op jit(solution)/shard_map/pallas_call | solution.py:419
  43.1 2.7 %shard_map.139 = (f32[3,16,32,512]{3,2,1,0:T(8,128)}, f32[3,16,32,512]{3,2,1,0:T(8,128)}, f32[1,16,24]{2,1,0:T(8,128)}, f32[8,128]{1,0:T(8,128)}) custom-call(f32[2,3,16,32,512]{4,3,2,1,0:T(8,128)S(1)} %get-tuple-element.7.E2, f32[1,16,24]{2,1,0:T(8,128)S(1)} %get-tuple-element.8.port, f32[8,128]{1,0:T(8,128)S(1)} %get-tuple-element.9.seg), custom_call_target="tpu_custom_call" | custom-call | tf_op jit(solution)/shard_map/pallas_call | solution.py:461

commit v2 on v1

--- a/solution.py
+++ b/solution.py
@@ -180,7 +180,7 @@
                 h_tile(r, phase, i, j, False)
             return carry
 
-        lax.fori_loop(0, CX - 1, body, 0)
+        lax.fori_loop(0, CX - 1, body, 0, unroll=5)
 
     def h_edge(r, phase):
         def body(i, carry):
@@ -194,7 +194,7 @@
         for n, c in enumerate((0, 2)):
             ysend[r, phase + 1, n, CX - 1] = H[r, c, CX - 1, pl.ds(CY - 1, 1), :]
         send(r, phase + 1, 0)
-        lax.fori_loop(0, CX - 1, body, 0)
+        lax.fori_loop(0, CX - 1, body, 0, unroll=5)
         send(r, phase + 1, 1)
 
     def e_inner(r, phase):
@@ -203,7 +203,7 @@
                 e_tile(r, phase, i, j, False)
             return carry
 
-        lax.fori_loop(1, CX, body, 0)
+        lax.fori_loop(1, CX, body, 0, unroll=5)
 
     def e_edge(r, phase):
         more = phase == 1
@@ -221,7 +221,7 @@
             for n, c in enumerate((0, 2)):
                 ysend[r, phase + 1, n, 0] = E[r, c, 0, pl.ds(0, 1), :]
             send(r, phase + 1, 0)
-        lax.fori_loop(1, CX, body, 0)
+        lax.fori_loop(1, CX, body, 0, unroll=5)
         if more:
             send(r, phase + 1, 1)
 
@@ -240,7 +240,7 @@
             pacc[n, :, pl.ds(t * ZBLK, ZBLK)] = total
             return carry
 
-        lax.fori_loop(0, mode.shape[0], body, 0)
+        lax.fori_loop(0, mode.shape[0], body, 0, unroll=4)
 
     def width_copies(d):
         to = lax.rem(w + d, n_width)

time: 46.1 us -> 37.1 us (0.80)
  Pallas kernels: 45.2 us -> 36.3 us
    pallas_call x1, Pallas kernels: 42.5 us -> 33.5 us  [on_device(): pl.pallas_call(functools.partial(kernel, n_prop, n_width), out_shape=(plt...]
where the time goes in v2:
time: 37.1 us; the launch traced here: 36.9 us
  Pallas kernels  36.3 us (98%)
  between operations  0.64 us (2%)
    pallas_call x1, Pallas kernels, on_device(): pl.pallas_call(functools.partial(kernel, n_prop, n_width), out_shape=(plt...  33.5 us
    pallas_call x1, Pallas kernels, on_device(): pl.pallas_call(write_out, out_shape=(jax.ShapeDtypeStruct(e_forward.shape...  2.74 us

profile of v2, /device:TPU:0, one launch (start us, length us, event | category | flops | bytes accessed | tf_op | source)
XLA Modules:
  0.0 36.9 jit_solution(15387997373737406668)
XLA Ops:
  0.6 33.5 %shard_map.138 = (f32[2,3,16,32,512]{4,3,2,1,0:T(8,128)S(1)}, f32[1,16,24]{2,1,0:T(8,128)S(1)}, f32[8,128]{1,0:T(8,128)S(1)}) custom-call(f32[3,16,32,512]{3,2,1,0:T(8,128)} %ef_in.1, f32[3,16,32,512]{3,2,1,0:T(8,128)} %hf_in.1, f32[3,16,32,512]{3,2,1,0:T(8,128)} %ea_in.1, f32[3,16,32,512]{3,2,1,0:T(8,128)} %ha_in.1, s32[16,32,512]{2,1,0:T(8,128)} %mat_in.1, ...), custom_call_target="tpu_custom_call" | custom-call | tf_op jit(solution)/shard_map/pallas_call | solution.py:419
  34.2 2.7 %shard_map.139 = (f32[3,16,32,512]{3,2,1,0:T(8,128)}, f32[3,16,32,512]{3,2,1,0:T(8,128)}, f32[1,16,24]{2,1,0:T(8,128)}, f32[8,128]{1,0:T(8,128)}) custom-call(f32[2,3,16,32,512]{4,3,2,1,0:T(8,128)S(1)} %get-tuple-element.7.E2, f32[1,16,24]{2,1,0:T(8,128)S(1)} %get-tuple-element.8.port, f32[8,128]{1,0:T(8,128)S(1)} %get-tuple-element.9.seg), custom_call_target="tpu_custom_call" | custom-call | tf_op jit(solution)/shard_map/pallas_call | solution.py:461
